TPU v7x, 128 devices: a whole 4x4x4 slice. The times are simulated.
128 devices in a mesh: gx: 16 (over z, y), gy: 8 (over x, core).
Axes of the slice: x: 4, y: 4, z: 4, core: 2. Of those that a mesh axis runs over, the one named last changes fastest.
Arguments:
- pumping: float32 [16, 4, 128, 1024], P(None, None, 'gx', 'gy'), may hold values from -1080 to 1080
- conductivity: float32 [4, 128, 1024], P(None, 'gx', 'gy'), may hold values from 0.2 to 5
- capacity: float32 [4, 128, 1024], P(None, 'gx', 'gy'), may hold values from 1 to 10
Outputs:
- solution: float32 [16, 4, 128, 1024], P(None, None, 'gx', 'gy')
- residual: float32 [16, 4, 128, 1024], P(None, None, 'gx', 'gy')
All inputs are finite; a program needn't handle non-finite values.
Results may differ from a plain program's by a relative error of at most 0.0035.
Values sent between devices are 32-bit elements; how exact they have to be, the bound alone decides.
A program may use at most 64 MiB of HBM per device.

v0:
```python
import jax
import jax.numpy as jnp
from jax import lax
from jax.sharding import PartitionSpec as P

RHS = 16
S = 4
CYCLES = 5
BASIS = 80


def padded_2(array, sides, width):
    for axis, dim in sides:
        devices, length = (lax.axis_size(axis), array.shape[dim])
        up = [(i, (i + 1) % devices) for i in range(devices - 1)]
        down = [(j, i) for i, j in up]
        last = lax.slice_in_dim(array, length - width, length, axis=dim)
        leading = lax.slice_in_dim(array, 0, width, axis=dim)
        before = lax.ppermute(last, axis, up)
        after = lax.ppermute(leading, axis, down)
        array = jnp.concatenate([before, array, after], axis=dim)
    return array


def halo_4(array):
    out = {}
    for axis, dim in (("gx", 2), ("gy", 3)):
        devices, length = (lax.axis_size(axis), array.shape[dim])
        up = [(i, (i + 1) % devices) for i in range(devices - 1)]
        down = [(j, i) for i, j in up]
        last = lax.slice_in_dim(array, length - 1, length, axis=dim)
        leading = lax.slice_in_dim(array, 0, 1, axis=dim)
        out[axis] = (lax.ppermute(last, axis, up), lax.ppermute(leading, axis, down))
    xb, xa = out["gx"]
    yb, ya = out["gy"]
    rows = jnp.concatenate([xb, array, xa], axis=2)
    zero_pad = ((0, 0), (0, 0), (1, 1), (0, 0))
    return jnp.concatenate([jnp.pad(yb, zero_pad), rows, jnp.pad(ya, zero_pad)], axis=3)


def face_terms(padded, storage):
    core = padded[1:-1, 1:-1, 1:-1]
    terms = (
        (core + padded[:-2, 1:-1, 1:-1]) * 0.5,
        (core + padded[2:, 1:-1, 1:-1]) * 0.5,
        (core + padded[1:-1, :-2, 1:-1]) * 0.5,
        (core + padded[1:-1, 2:, 1:-1]) * 0.5,
        (core + padded[1:-1, 1:-1, :-2]) * 0.5,
        (core + padded[1:-1, 1:-1, 2:]) * 0.5,
    )
    diagonal = storage + terms[0] + terms[1] + terms[2] + terms[3] + terms[4] + terms[5]
    return (terms, diagonal)


def apply_off(padded, terms):
    total = terms[0] * padded[:, :-2, 1:-1, 1:-1] + terms[1] * padded[:, 2:, 1:-1, 1:-1]
    total = total + terms[2] * padded[:, 1:-1, :-2, 1:-1] + terms[3] * padded[:, 1:-1, 2:, 1:-1]
    total = total + terms[4] * padded[:, 1:-1, 1:-1, :-2] + terms[5] * padded[:, 1:-1, 1:-1, 2:]
    return total


def small_solve(gram_all):
    shift_matrix = jnp.eye(BASIS, BASIS - RHS, dtype=jnp.float32) + jnp.eye(
        BASIS, BASIS - RHS, k=-RHS, dtype=jnp.float32
    )
    first_block = jnp.eye(BASIS, RHS, dtype=jnp.float32)
    hp = lax.Precision.HIGHEST
    gram_shift = jnp.dot(gram_all, shift_matrix, precision=hp)
    normal = jnp.dot(shift_matrix.T, gram_shift, precision=hp)
    right_side = jnp.dot(gram_shift.T, first_block, precision=hp)
    lower = jnp.linalg.cholesky(normal)
    y = jax.scipy.linalg.cho_solve((lower, True), right_side)
    coeffs = first_block - jnp.dot(shift_matrix, y, precision=hp)
    return (y, coeffs)


def shards(pumping, conductivity, capacity):
    hp = lax.Precision.HIGHEST
    shape = pumping.shape
    cond_halo = padded_2(conductivity, (("gx", 1), ("gy", 2)), 1)
    cond_pad = jnp.pad(cond_halo, ((1, 1), (0, 0), (0, 0)))
    terms, diagonal = face_terms(cond_pad, capacity)
    solution = jnp.zeros(shape, jnp.float32)
    residual = pumping / diagonal
    for restart in range(CYCLES):
        blocks = [residual]
        for k in range(S):
            bordered = halo_4(blocks[-1])
            padded = jnp.pad(bordered, ((0, 0), (1, 1), (0, 0), (0, 0)))
            blocks.append(-apply_off(padded, terms) / diagonal)
        stacked = jnp.concatenate(blocks, 0).reshape(BASIS, -1)
        local_gram = jnp.dot(stacked, stacked.T, precision=hp)
        gram_all = lax.psum(local_gram, ("gx", "gy"))
        y, coeffs = small_solve(gram_all)
        solution = solution + jnp.dot(y.T, stacked[: BASIS - RHS], precision=hp).reshape(shape)
        residual = jnp.dot(coeffs.T, stacked, precision=hp).reshape(shape)
    return (solution, residual)


def solution(mesh):
    return jax.shard_map(
        shards,
        mesh=mesh,
        in_specs=(P(None, None, "gx", "gy"), P(None, "gx", "gy"), P(None, "gx", "gy")),
        out_specs=(P(None, None, "gx", "gy"), P(None, None, "gx", "gy")),
        check_vma=False,
    )
```

profile of v0, /device:TPU:1, one launch (start us, length us, event | category | flops | bytes accessed | tf_op | source)
XLA Modules:
  0.0 819.0 jit_solution(14355877820562168291)
XLA Ops:
  10.6 5.1 collective-permute-start.2
  34.1 4.4 collective-permute-done.7
  50.4 4.4 collective-permute-done.11
  55.6 5.2 collective-permute-start.13
  67.6 4.4 collective-permute-done.15
  72.9 4.3 collective-permute-start.17
  83.9 4.4 collective-permute-done.19
  90.7 75.5 %psum.35 = f32[80,80]{1,0:T(8,128)S(1)} all-reduce(f32[80,80]{1,0:T(8,128)S(1)} %convolution_bitcast_fusion.4), channel_id=1, replica_groups=mesh['gx'=16,'gy'=8] {'gx','gy'}, use_global_device_ids=true, to_apply=%region_0.1 | all-reduce | flops 6400 | bytes 51200 | tf_op jit(solution)/shard_map/psum | solution.py:93
  168.1 5.8 cholesky.89
  175.3 4.9 custom-call.11
  192.7 4.4 collective-permute-done.23
  209.0 4.4 collective-permute-done.27
  225.2 4.4 collective-permute-done.31
  241.5 4.4 collective-permute-done.35
  249.4 73.8 %psum.36 = f32[80,80]{1,0:T(8,128)S(1)} all-reduce(f32[80,80]{1,0:T(8,128)S(1)} %convolution_bitcast_fusion.3), channel_id=1, replica_groups=mesh['gx'=16,'gy'=8] {'gx','gy'}, use_global_device_ids=true, to_apply=%region_3.6 | all-reduce | flops 6400 | bytes 51200 | tf_op jit(solution)/shard_map/psum | solution.py:93
  327.5 5.8 cholesky.100
  334.7 4.9 custom-call.12
  352.9 4.4 collective-permute-done.39
  369.2 4.4 collective-permute-done.43
  385.5 4.4 collective-permute-done.47
  390.9 4.5 collective-permute-start.49
  409.9 73.9 %psum.37 = f32[80,80]{1,0:T(8,128)S(1)} all-reduce(f32[80,80]{1,0:T(8,128)S(1)} %convolution_bitcast_fusion.2), channel_id=1, replica_groups=mesh['gx'=16,'gy'=8] {'gx','gy'}, use_global_device_ids=true, to_apply=%region_4.7 | all-reduce | flops 6400 | bytes 51200 | tf_op jit(solution)/shard_map/psum | solution.py:93
  488.1 5.8 cholesky.111
  495.3 4.9 custom-call.13
  506.5 4.3 collective-permute-start.52
  569.8 73.8 %psum.38 = f32[80,80]{1,0:T(8,128)S(1)} all-reduce(f32[80,80]{1,0:T(8,128)S(1)} %convolution_bitcast_fusion.1), channel_id=1, replica_groups=mesh['gx'=16,'gy'=8] {'gx','gy'}, use_global_device_ids=true, to_apply=%region_5.8 | all-reduce | flops 6400 | bytes 51200 | tf_op jit(solution)/shard_map/psum | solution.py:93
  645.5 5.8 cholesky.122
  652.7 4.9 custom-call.14
  670.0 4.4 collective-permute-done.71
  725.7 74.1 %psum.39 = f32[80,80]{1,0:T(8,128)S(1)} all-reduce(f32[80,80]{1,0:T(8,128)S(1)} %convolution_bitcast_fusion), channel_id=1, replica_groups=mesh['gx'=16,'gy'=8] {'gx','gy'}, use_global_device_ids=true, to_apply=%region_6.9 | all-reduce | flops 6400 | bytes 51200 | tf_op jit(solution)/shard_map/psum | solution.py:93
  801.7 5.8 cholesky.133
  808.9 4.9 custom-call.15
  (389 shorter events, 315.0 us)
Async XLA Ops:
  23.9 14.6 %collective-permute-start.5 = (f32[16,4,1,128]{3,0,2,1:T(8,128)S(1)}, f32[16,4,1,128]{3,0,2,1:T(8,128)S(1)}, u32[]{:S(2)}, u32[]{:S(2)}) collective-permute-start(f32[16,4,1,128]{3,0,2,1:T(8,128)S(1)} %get-tuple-element.125), channel_id=1, source_target_pairs={{0,8},{8,16},{16,24},{24,32},{32,40},{40,48},{48,56},{56,64},{64,7... | collective-permute-start | bytes 98312 | tf_op jit(solution)/shard_map/ppermute | solution.py:33
  27.1 11.4 %collective-permute-start.6 = (f32[16,4,1,128]{3,0,2,1:T(8,128)S(1)}, f32[16,4,1,128]{3,0,2,1:T(8,128)S(1)}, u32[]{:S(2)}, u32[]{:S(2)}) collective-permute-start(f32[16,4,1,128]{3,0,2,1:T(8,128)S(1)} %get-tuple-element.126), channel_id=1, source_target_pairs={{8,0},{16,8},{24,16},{32,24},{40,32},{48,40},{56,48},{64,56},{72,6... | collective-permute-start | bytes 98312 | tf_op jit(solution)/shard_map/ppermute | solution.py:33
  39.3 15.5 %collective-permute-start.9 = (f32[16,4,1,128]{3,0,2,1:T(8,128)S(1)}, f32[16,4,1,128]{3,0,2,1:T(8,128)S(1)}, u32[]{:S(2)}, u32[]{:S(2)}) collective-permute-start(f32[16,4,1,128]{3,0,2,1:T(8,128)S(1)} %get-tuple-element.121), channel_id=1, source_target_pairs={{0,8},{8,16},{16,24},{24,32},{32,40},{40,48},{48,56},{56,64},{64,7... | collective-permute-start | bytes 98312 | tf_op jit(solution)/shard_map/ppermute | solution.py:33
  43.6 11.2 %collective-permute-start.10 = (f32[16,4,1,128]{3,0,2,1:T(8,128)S(1)}, f32[16,4,1,128]{3,0,2,1:T(8,128)S(1)}, u32[]{:S(2)}, u32[]{:S(2)}) collective-permute-start(f32[16,4,1,128]{3,0,2,1:T(8,128)S(1)} %get-tuple-element.122), channel_id=1, source_target_pairs={{8,0},{16,8},{24,16},{32,24},{40,32},{48,40},{56,48},{64,56},{72,6... | collective-permute-start | bytes 98312 | tf_op jit(solution)/shard_map/ppermute | solution.py:33
  55.6 16.4 %collective-permute-start.13 = (f32[16,4,1,128]{3,0,2,1:T(8,128)S(1)}, f32[16,4,1,128]{3,0,2,1:T(8,128)S(1)}, u32[]{:S(2)}, u32[]{:S(2)}) collective-permute-start(f32[16,4,1,128]{3,0,2,1:T(8,128)S(1)} %get-tuple-element.117), channel_id=1, source_target_pairs={{0,8},{8,16},{16,24},{24,32},{32,40},{40,48},{48,56},{56,64},{64,7... | collective-permute-start | bytes 98312 | tf_op jit(solution)/shard_map/ppermute | solution.py:33
  60.8 11.2 %collective-permute-start.14 = (f32[16,4,1,128]{3,0,2,1:T(8,128)S(1)}, f32[16,4,1,128]{3,0,2,1:T(8,128)S(1)}, u32[]{:S(2)}, u32[]{:S(2)}) collective-permute-start(f32[16,4,1,128]{3,0,2,1:T(8,128)S(1)} %get-tuple-element.118), channel_id=1, source_target_pairs={{8,0},{16,8},{24,16},{32,24},{40,32},{48,40},{56,48},{64,56},{72,6... | collective-permute-start | bytes 98312 | tf_op jit(solution)/shard_map/ppermute | solution.py:33
  72.9 15.3 %collective-permute-start.17 = (f32[16,4,1,128]{3,0,2,1:T(8,128)S(1)}, f32[16,4,1,128]{3,0,2,1:T(8,128)S(1)}, u32[]{:S(2)}, u32[]{:S(2)}) collective-permute-start(f32[16,4,1,128]{3,0,2,1:T(8,128)S(1)} %get-tuple-element.113), channel_id=1, source_target_pairs={{0,8},{8,16},{16,24},{24,32},{32,40},{40,48},{48,56},{56,64},{64,7... | collective-permute-start | bytes 98312 | tf_op jit(solution)/shard_map/ppermute | solution.py:33
  182.4 14.7 %collective-permute-start.21 = (f32[16,4,1,128]{3,0,2,1:T(8,128)S(1)}, f32[16,4,1,128]{3,0,2,1:T(8,128)S(1)}, u32[]{:S(2)}, u32[]{:S(2)}) collective-permute-start(f32[16,4,1,128]{3,0,2,1:T(8,128)S(1)} %get-tuple-element.109), channel_id=1, source_target_pairs={{0,8},{8,16},{16,24},{24,32},{32,40},{40,48},{48,56},{56,64},{64,7... | collective-permute-start | bytes 98312 | tf_op jit(solution)/shard_map/ppermute | solution.py:33
  184.1 13.0 %collective-permute-start.22 = (f32[16,4,1,128]{3,0,2,1:T(8,128)S(1)}, f32[16,4,1,128]{3,0,2,1:T(8,128)S(1)}, u32[]{:S(2)}, u32[]{:S(2)}) collective-permute-start(f32[16,4,1,128]{3,0,2,1:T(8,128)S(1)} %get-tuple-element.110), channel_id=1, source_target_pairs={{8,0},{16,8},{24,16},{32,24},{40,32},{48,40},{56,48},{64,56},{72,6... | collective-permute-start | bytes 98312 | tf_op jit(solution)/shard_map/ppermute | solution.py:33
  197.9 15.5 %collective-permute-start.25 = (f32[16,4,1,128]{3,0,2,1:T(8,128)S(1)}, f32[16,4,1,128]{3,0,2,1:T(8,128)S(1)}, u32[]{:S(2)}, u32[]{:S(2)}) collective-permute-start(f32[16,4,1,128]{3,0,2,1:T(8,128)S(1)} %get-tuple-element.105), channel_id=1, source_target_pairs={{0,8},{8,16},{16,24},{24,32},{32,40},{40,48},{48,56},{56,64},{64,7... | collective-permute-start | bytes 98312 | tf_op jit(solution)/shard_map/ppermute | solution.py:33
  202.2 11.2 %collective-permute-start.26 = (f32[16,4,1,128]{3,0,2,1:T(8,128)S(1)}, f32[16,4,1,128]{3,0,2,1:T(8,128)S(1)}, u32[]{:S(2)}, u32[]{:S(2)}) collective-permute-start(f32[16,4,1,128]{3,0,2,1:T(8,128)S(1)} %get-tuple-element.106), channel_id=1, source_target_pairs={{8,0},{16,8},{24,16},{32,24},{40,32},{48,40},{56,48},{64,56},{72,6... | collective-permute-start | bytes 98312 | tf_op jit(solution)/shard_map/ppermute | solution.py:33
  214.2 15.5 %collective-permute-start.29 = (f32[16,4,1,128]{3,0,2,1:T(8,128)S(1)}, f32[16,4,1,128]{3,0,2,1:T(8,128)S(1)}, u32[]{:S(2)}, u32[]{:S(2)}) collective-permute-start(f32[16,4,1,128]{3,0,2,1:T(8,128)S(1)} %get-tuple-element.101), channel_id=1, source_target_pairs={{0,8},{8,16},{16,24},{24,32},{32,40},{40,48},{48,56},{56,64},{64,7... | collective-permute-start | bytes 98312 | tf_op jit(solution)/shard_map/ppermute | solution.py:33
  218.4 11.2 %collective-permute-start.30 = (f32[16,4,1,128]{3,0,2,1:T(8,128)S(1)}, f32[16,4,1,128]{3,0,2,1:T(8,128)S(1)}, u32[]{:S(2)}, u32[]{:S(2)}) collective-permute-start(f32[16,4,1,128]{3,0,2,1:T(8,128)S(1)} %get-tuple-element.102), channel_id=1, source_target_pairs={{8,0},{16,8},{24,16},{32,24},{40,32},{48,40},{56,48},{64,56},{72,6... | collective-permute-start | bytes 98312 | tf_op jit(solution)/shard_map/ppermute | solution.py:33
  230.5 15.5 %collective-permute-start.33 = (f32[16,4,1,128]{3,0,2,1:T(8,128)S(1)}, f32[16,4,1,128]{3,0,2,1:T(8,128)S(1)}, u32[]{:S(2)}, u32[]{:S(2)}) collective-permute-start(f32[16,4,1,128]{3,0,2,1:T(8,128)S(1)} %get-tuple-element.97), channel_id=1, source_target_pairs={{0,8},{8,16},{16,24},{24,32},{32,40},{40,48},{48,56},{56,64},{64,7... | collective-permute-start | bytes 98312 | tf_op jit(solution)/shard_map/ppermute | solution.py:33
  234.7 11.2 %collective-permute-start.34 = (f32[16,4,1,128]{3,0,2,1:T(8,128)S(1)}, f32[16,4,1,128]{3,0,2,1:T(8,128)S(1)}, u32[]{:S(2)}, u32[]{:S(2)}) collective-permute-start(f32[16,4,1,128]{3,0,2,1:T(8,128)S(1)} %get-tuple-element.98), channel_id=1, source_target_pairs={{8,0},{16,8},{24,16},{32,24},{40,32},{48,40},{56,48},{64,56},{72,6... | collective-permute-start | bytes 98312 | tf_op jit(solution)/shard_map/ppermute | solution.py:33
  343.1 14.3 %collective-permute-start.37 = (f32[16,4,1,128]{3,0,2,1:T(8,128)S(1)}, f32[16,4,1,128]{3,0,2,1:T(8,128)S(1)}, u32[]{:S(2)}, u32[]{:S(2)}) collective-permute-start(f32[16,4,1,128]{3,0,2,1:T(8,128)S(1)} %get-tuple-element.93), channel_id=1, source_target_pairs={{0,8},{8,16},{16,24},{24,32},{32,40},{40,48},{48,56},{56,64},{64,7... | collective-permute-start | bytes 98312 | tf_op jit(solution)/shard_map/ppermute | solution.py:33
  344.4 13.0 %collective-permute-start.38 = (f32[16,4,1,128]{3,0,2,1:T(8,128)S(1)}, f32[16,4,1,128]{3,0,2,1:T(8,128)S(1)}, u32[]{:S(2)}, u32[]{:S(2)}) collective-permute-start(f32[16,4,1,128]{3,0,2,1:T(8,128)S(1)} %get-tuple-element.94), channel_id=1, source_target_pairs={{8,0},{16,8},{24,16},{32,24},{40,32},{48,40},{56,48},{64,56},{72,6... | collective-permute-start | bytes 98312 | tf_op jit(solution)/shard_map/ppermute | solution.py:33
  358.2 15.5 %collective-permute-start.41 = (f32[16,4,1,128]{3,0,2,1:T(8,128)S(1)}, f32[16,4,1,128]{3,0,2,1:T(8,128)S(1)}, u32[]{:S(2)}, u32[]{:S(2)}) collective-permute-start(f32[16,4,1,128]{3,0,2,1:T(8,128)S(1)} %get-tuple-element.89), channel_id=1, source_target_pairs={{0,8},{8,16},{16,24},{24,32},{32,40},{40,48},{48,56},{56,64},{64,7... | collective-permute-start | bytes 98312 | tf_op jit(solution)/shard_map/ppermute | solution.py:33
  362.4 11.2 %collective-permute-start.42 = (f32[16,4,1,128]{3,0,2,1:T(8,128)S(1)}, f32[16,4,1,128]{3,0,2,1:T(8,128)S(1)}, u32[]{:S(2)}, u32[]{:S(2)}) collective-permute-start(f32[16,4,1,128]{3,0,2,1:T(8,128)S(1)} %get-tuple-element.90), channel_id=1, source_target_pairs={{8,0},{16,8},{24,16},{32,24},{40,32},{48,40},{56,48},{64,56},{72,6... | collective-permute-start | bytes 98312 | tf_op jit(solution)/shard_map/ppermute | solution.py:33
  374.4 15.5 %collective-permute-start.45 = (f32[16,4,1,128]{3,0,2,1:T(8,128)S(1)}, f32[16,4,1,128]{3,0,2,1:T(8,128)S(1)}, u32[]{:S(2)}, u32[]{:S(2)}) collective-permute-start(f32[16,4,1,128]{3,0,2,1:T(8,128)S(1)} %get-tuple-element.85), channel_id=1, source_target_pairs={{0,8},{8,16},{16,24},{24,32},{32,40},{40,48},{48,56},{56,64},{64,7... | collective-permute-start | bytes 98312 | tf_op jit(solution)/shard_map/ppermute | solution.py:33
  378.7 11.2 %collective-permute-start.46 = (f32[16,4,1,128]{3,0,2,1:T(8,128)S(1)}, f32[16,4,1,128]{3,0,2,1:T(8,128)S(1)}, u32[]{:S(2)}, u32[]{:S(2)}) collective-permute-start(f32[16,4,1,128]{3,0,2,1:T(8,128)S(1)} %get-tuple-element.86), channel_id=1, source_target_pairs={{8,0},{16,8},{24,16},{32,24},{40,32},{48,40},{56,48},{64,56},{72,6... | collective-permute-start | bytes 98312 | tf_op jit(solution)/shard_map/ppermute | solution.py:33
  390.9 15.5 %collective-permute-start.49 = (f32[16,4,1,128]{3,0,2,1:T(8,128)S(1)}, f32[16,4,1,128]{3,0,2,1:T(8,128)S(1)}, u32[]{:S(2)}, u32[]{:S(2)}) collective-permute-start(f32[16,4,1,128]{3,0,2,1:T(8,128)S(1)} %get-tuple-element.81), channel_id=1, source_target_pairs={{0,8},{8,16},{16,24},{24,32},{32,40},{40,48},{48,56},{56,64},{64,7... | collective-permute-start | bytes 98312 | tf_op jit(solution)/shard_map/ppermute | solution.py:33
  503.9 14.7 %collective-permute-start.53 = (f32[16,4,1,128]{3,0,2,1:T(8,128)S(1)}, f32[16,4,1,128]{3,0,2,1:T(8,128)S(1)}, u32[]{:S(2)}, u32[]{:S(2)}) collective-permute-start(f32[16,4,1,128]{3,0,2,1:T(8,128)S(1)} %get-tuple-element.77), channel_id=1, source_target_pairs={{0,8},{8,16},{16,24},{24,32},{32,40},{40,48},{48,56},{56,64},{64,7... | collective-permute-start | bytes 98312 | tf_op jit(solution)/shard_map/ppermute | solution.py:33
  505.2 13.4 %collective-permute-start.54 = (f32[16,4,1,128]{3,0,2,1:T(8,128)S(1)}, f32[16,4,1,128]{3,0,2,1:T(8,128)S(1)}, u32[]{:S(2)}, u32[]{:S(2)}) collective-permute-start(f32[16,4,1,128]{3,0,2,1:T(8,128)S(1)} %get-tuple-element.78), channel_id=1, source_target_pairs={{8,0},{16,8},{24,16},{32,24},{40,32},{48,40},{56,48},{64,56},{72,6... | collective-permute-start | bytes 98312 | tf_op jit(solution)/shard_map/ppermute | solution.py:33
  519.5 15.3 %collective-permute-start.57 = (f32[16,4,1,128]{3,0,2,1:T(8,128)S(1)}, f32[16,4,1,128]{3,0,2,1:T(8,128)S(1)}, u32[]{:S(2)}, u32[]{:S(2)}) collective-permute-start(f32[16,4,1,128]{3,0,2,1:T(8,128)S(1)} %get-tuple-element.73), channel_id=1, source_target_pairs={{0,8},{8,16},{16,24},{24,32},{32,40},{40,48},{48,56},{56,64},{64,7... | collective-permute-start | bytes 98312 | tf_op jit(solution)/shard_map/ppermute | solution.py:33
  535.8 15.3 %collective-permute-start.61 = (f32[16,4,1,128]{3,0,2,1:T(8,128)S(1)}, f32[16,4,1,128]{3,0,2,1:T(8,128)S(1)}, u32[]{:S(2)}, u32[]{:S(2)}) collective-permute-start(f32[16,4,1,128]{3,0,2,1:T(8,128)S(1)} %get-tuple-element.69), channel_id=1, source_target_pairs={{0,8},{8,16},{16,24},{24,32},{32,40},{40,48},{48,56},{56,64},{64,7... | collective-permute-start | bytes 98312 | tf_op jit(solution)/shard_map/ppermute | solution.py:33
  552.1 15.3 %collective-permute-start.65 = (f32[16,4,1,128]{3,0,2,1:T(8,128)S(1)}, f32[16,4,1,128]{3,0,2,1:T(8,128)S(1)}, u32[]{:S(2)}, u32[]{:S(2)}) collective-permute-start(f32[16,4,1,128]{3,0,2,1:T(8,128)S(1)} %get-tuple-element.65), channel_id=1, source_target_pairs={{0,8},{8,16},{16,24},{24,32},{32,40},{40,48},{48,56},{56,64},{64,7... | collective-permute-start | bytes 98312 | tf_op jit(solution)/shard_map/ppermute | solution.py:33
  660.0 14.4 %collective-permute-start.69 = (f32[16,4,1,128]{3,0,2,1:T(8,128)S(1)}, f32[16,4,1,128]{3,0,2,1:T(8,128)S(1)}, u32[]{:S(2)}, u32[]{:S(2)}) collective-permute-start(f32[16,4,1,128]{3,0,2,1:T(8,128)S(1)} %get-tuple-element.61), channel_id=1, source_target_pairs={{0,8},{8,16},{16,24},{24,32},{32,40},{40,48},{48,56},{56,64},{64,7... | collective-permute-start | bytes 98312 | tf_op jit(solution)/shard_map/ppermute | solution.py:33
  661.3 13.2 %collective-permute-start.70 = (f32[16,4,1,128]{3,0,2,1:T(8,128)S(1)}, f32[16,4,1,128]{3,0,2,1:T(8,128)S(1)}, u32[]{:S(2)}, u32[]{:S(2)}) collective-permute-start(f32[16,4,1,128]{3,0,2,1:T(8,128)S(1)} %get-tuple-element.62), channel_id=1, source_target_pairs={{8,0},{16,8},{24,16},{32,24},{40,32},{48,40},{56,48},{64,56},{72,6... | collective-permute-start | bytes 98312 | tf_op jit(solution)/shard_map/ppermute | solution.py:33
  675.4 15.3 %collective-permute-start.73 = (f32[16,4,1,128]{3,0,2,1:T(8,128)S(1)}, f32[16,4,1,128]{3,0,2,1:T(8,128)S(1)}, u32[]{:S(2)}, u32[]{:S(2)}) collective-permute-start(f32[16,4,1,128]{3,0,2,1:T(8,128)S(1)} %get-tuple-element.57), channel_id=1, source_target_pairs={{0,8},{8,16},{16,24},{24,32},{32,40},{40,48},{48,56},{56,64},{64,7... | collective-permute-start | bytes 98312 | tf_op jit(solution)/shard_map/ppermute | solution.py:33
  691.6 15.3 %collective-permute-start.77 = (f32[16,4,1,128]{3,0,2,1:T(8,128)S(1)}, f32[16,4,1,128]{3,0,2,1:T(8,128)S(1)}, u32[]{:S(2)}, u32[]{:S(2)}) collective-permute-start(f32[16,4,1,128]{3,0,2,1:T(8,128)S(1)} %get-tuple-element.53), channel_id=1, source_target_pairs={{0,8},{8,16},{16,24},{24,32},{32,40},{40,48},{48,56},{56,64},{64,7... | collective-permute-start | bytes 98312 | tf_op jit(solution)/shard_map/ppermute | solution.py:33
  707.9 15.3 %collective-permute-start.81 = (f32[16,4,1,128]{3,0,2,1:T(8,128)S(1)}, f32[16,4,1,128]{3,0,2,1:T(8,128)S(1)}, u32[]{:S(2)}, u32[]{:S(2)}) collective-permute-start(f32[16,4,1,128]{3,0,2,1:T(8,128)S(1)} %get-tuple-element.49), channel_id=1, source_target_pairs={{0,8},{8,16},{16,24},{24,32},{32,40},{40,48},{48,56},{56,64},{64,7... | collective-permute-start | bytes 98312 | tf_op jit(solution)/shard_map/ppermute | solution.py:33
  (54 other events, 407.3 us)
where the time goes:
time: 827 us; the launch traced here: 819 us
  blocking collectives  371 us (45%)
  starting transfers between devices  206 us (25%)
  waiting for transfers between devices  99.7 us (12%)
  other arithmetic  80.1 us (10%)
  local copies, waits for them, and re-layouts  29.8 us (4%)
  matrix products  28.9 us (3%)
    psum x5, blocking collectives, shards(): gram_all = lax.psum(local_gram, ('gx', 'gy'))  371 us
    ppermute x40, starting transfers between devices, halo_4(): lax.ppermute(last, axis, up)  123 us
    ppermute x40, waiting for transfers between devices, halo_4(): lax.ppermute(leading, axis, down)  81.7 us
    ppermute x40, starting transfers between devices, halo_4(): lax.ppermute(leading, axis, down)  71.1 us
    another operation x15, other arithmetic, small_solve(): lower = jnp.linalg.cholesky(normal)  32.6 us
    another operation x10, other arithmetic, small_solve(): y = jax.scipy.linalg.cho_solve((lower, True), right_side)  27.7 us
    unnamed x26, local copies, waits for them, and re-layouts  17.6 us
  transfers between devices with their start and end apart: 84, of which 34 were waited for; matrix products, arithmetic and copies ran while one was open for 2% of the time, Pallas kernels for 0%

commit v1 on v0

--- a/solution.py
+++ b/solution.py
@@ -90,7 +90,8 @@
             blocks.append(-apply_off(padded, terms) / diagonal)
         stacked = jnp.concatenate(blocks, 0).reshape(BASIS, -1)
         local_gram = jnp.dot(stacked, stacked.T, precision=hp)
-        gram_all = lax.psum(local_gram, ("gx", "gy"))
+        shards_2 = lax.all_gather(local_gram, ("gx", "gy"))
+        gram_all = jnp.sum(shards_2, axis=0)
         y, coeffs = small_solve(gram_all)
         solution = solution + jnp.dot(y.T, stacked[: BASIS - RHS], precision=hp).reshape(shape)
         residual = jnp.dot(coeffs.T, stacked, precision=hp).reshape(shape)

time: 827 us -> 849 us (1.027)
  blocking collectives: 371 us -> 0 us
  waiting for transfers between devices: 99.7 us -> 463 us
  other arithmetic: 80.1 us -> 95.2 us
  between operations: 3.35 us -> 16.7 us
    psum x5 -> x0, blocking collectives: 371 us -> none  [shards(): gram_all = lax.psum(local_gram, ('gx', 'gy'))]
    all_gather x0 -> x5, waiting for transfers between devices: none -> 348 us  [shards(): shards_2 = lax.all_gather(local_gram, ('gx', 'gy'))]
    reduce_sum x0 -> x5, other arithmetic: none -> 14.5 us  [shards(): gram_all = jnp.sum(shards_2, axis=0)]
    ppermute x40, waiting for transfers between devices: 11.8 us -> 21.1 us  [halo_4(): lax.ppermute(last, axis, up)]
    unnamed x26 -> x74, local copies, waits for them, and re-layouts: 17.6 us -> 17.4 us
  transfers between devices with their start and end apart: 84 -> 89, of which waited for: 34 -> 47; matrix products, arithmetic and copies ran while one was open for 2% -> 4% of each run, Pallas kernels for 0% -> 0%
where the time goes in v1:
time: 849 us; the launch traced here: 841 us
  waiting for transfers between devices  463 us (55%)
  starting transfers between devices  203 us (24%)
  other arithmetic  95.2 us (11%)
  matrix products  35.4 us (4%)
  local copies, waits for them, and re-layouts  27.5 us (3%)
  between operations  16.7 us (2%)
    all_gather x5, waiting for transfers between devices, shards(): shards_2 = lax.all_gather(local_gram, ('gx', 'gy'))  348 us
    ppermute x40, starting transfers between devices, halo_4(): lax.ppermute(last, axis, up)  119 us
    ppermute x40, waiting for transfers between devices, halo_4(): lax.ppermute(leading, axis, down)  87.4 us
    ppermute x40, starting transfers between devices, halo_4(): lax.ppermute(leading, axis, down)  70.5 us
    another operation x15, other arithmetic, small_solve(): lower = jnp.linalg.cholesky(normal)  32.6 us
    another operation x10, other arithmetic, small_solve(): y = jax.scipy.linalg.cho_solve((lower, True), right_side)  27.4 us
    ppermute x40, waiting for transfers between devices, halo_4(): lax.ppermute(last, axis, up)  21.1 us
    unnamed x74, local copies, waits for them, and re-layouts  17.4 us
  transfers between devices with their start and end apart: 89, of which 47 were waited for; matrix products, arithmetic and copies ran while one was open for 4% of the time, Pallas kernels for 0%

profile of v1, /device:TPU:1, one launch (start us, length us, event | category | flops | bytes accessed | tf_op | source)
XLA Modules:
  0.0 840.8 jit_solution(17181096815266075589)
XLA Ops:
  17.2 5.1 collective-permute-start.2
  56.9 4.4 collective-permute-done.11
  62.2 5.2 collective-permute-start.13
  74.2 4.4 collective-permute-done.15
  100.7 72.9 %all-gather.11.cloned.1.call-done = f32[10240,80]{1,0:T(8,128)} async-done(((f32[80,80]{1,0:T(8,128)}), f32[10240,80]{1,0:T(8,128)}) %all-gather.11.cloned.1.call-update) | async-done | bytes 3276816 | tf_op jit(solution)/shard_map/all_gather | solution.py:93
  177.4 5.8 cholesky.89
  184.5 4.9 custom-call.11
  202.2 4.4 collective-permute-done.23
  218.5 4.4 collective-permute-done.27
  234.8 4.4 collective-permute-done.31
  251.1 4.4 collective-permute-done.35
  261.0 72.4 %all-gather.13.cloned.1.call-done = f32[10240,80]{1,0:T(8,128)} async-done(((f32[80,80]{1,0:T(8,128)}), f32[10240,80]{1,0:T(8,128)}) %all-gather.13.cloned.1.call-update) | async-done | bytes 3276816 | tf_op jit(solution)/shard_map/all_gather | solution.py:93
  337.2 5.8 cholesky.100
  344.3 4.9 custom-call.12
  362.0 4.4 collective-permute-done.39
  378.3 4.4 collective-permute-done.43
  394.6 4.4 collective-permute-done.47
  410.9 4.4 collective-permute-done.51
  420.8 72.4 %all-gather.15.cloned.1.call-done = f32[10240,80]{1,0:T(8,128)} async-done(((f32[80,80]{1,0:T(8,128)}), f32[10240,80]{1,0:T(8,128)}) %all-gather.15.cloned.1.call-update) | async-done | bytes 3276816 | tf_op jit(solution)/shard_map/all_gather | solution.py:93
  497.0 5.8 cholesky.111
  504.1 4.9 custom-call.13
  521.8 4.4 collective-permute-done.55
  538.1 4.4 collective-permute-done.59
  554.4 4.4 collective-permute-done.63
  570.7 4.4 collective-permute-done.67
  580.8 72.2 %all-gather.17.cloned.1.call-done = f32[10240,80]{1,0:T(8,128)} async-done(((f32[80,80]{1,0:T(8,128)}), f32[10240,80]{1,0:T(8,128)}) %all-gather.17.cloned.1.call-update) | async-done | bytes 3276816 | tf_op jit(solution)/shard_map/all_gather | solution.py:93
  656.8 5.8 cholesky.122
  663.9 4.9 custom-call.14
  681.9 4.4 collective-permute-done.71
  755.4 57.8 %all-gather.19.cloned.1.call-done = f32[10240,80]{1,0:T(8,128)} async-done(((f32[80,80]{1,0:T(8,128)}), f32[10240,80]{1,0:T(8,128)}) %all-gather.19.cloned.1.call-update) | async-done | bytes 3276816 | tf_op jit(solution)/shard_map/all_gather | solution.py:93
  817.0 5.8 cholesky.133
  824.2 4.9 custom-call.15
  (452 shorter events, 346.8 us)
Async XLA Ops:
  7.2 166.5 %all-gather.11.cloned.1.call-start = ((), (), s32[]{:S(2)}) async-start(), calls=%async_computation | async-start | bytes 5283840 | tf_op jit(solution)/shard_map/all_gather | solution.py:93
  30.5 14.6 %collective-permute-start.5 = (f32[16,4,1,128]{3,0,2,1:T(8,128)S(1)}, f32[16,4,1,128]{3,0,2,1:T(8,128)S(1)}, u32[]{:S(2)}, u32[]{:S(2)}) collective-permute-start(f32[16,4,1,128]{3,0,2,1:T(8,128)S(1)} %get-tuple-element.125), channel_id=1, source_target_pairs={{0,8},{8,16},{16,24},{24,32},{32,40},{40,48},{48,56},{56,64},{64,7... | collective-permute-start | bytes 98312 | tf_op jit(solution)/shard_map/ppermute | solution.py:33
  33.7 11.4 %collective-permute-start.6 = (f32[16,4,1,128]{3,0,2,1:T(8,128)S(1)}, f32[16,4,1,128]{3,0,2,1:T(8,128)S(1)}, u32[]{:S(2)}, u32[]{:S(2)}) collective-permute-start(f32[16,4,1,128]{3,0,2,1:T(8,128)S(1)} %get-tuple-element.126), channel_id=1, source_target_pairs={{8,0},{16,8},{24,16},{32,24},{40,32},{48,40},{56,48},{64,56},{72,6... | collective-permute-start | bytes 98312 | tf_op jit(solution)/shard_map/ppermute | solution.py:33
  45.9 15.5 %collective-permute-start.9 = (f32[16,4,1,128]{3,0,2,1:T(8,128)S(1)}, f32[16,4,1,128]{3,0,2,1:T(8,128)S(1)}, u32[]{:S(2)}, u32[]{:S(2)}) collective-permute-start(f32[16,4,1,128]{3,0,2,1:T(8,128)S(1)} %get-tuple-element.121), channel_id=1, source_target_pairs={{0,8},{8,16},{16,24},{24,32},{32,40},{40,48},{48,56},{56,64},{64,7... | collective-permute-start | bytes 98312 | tf_op jit(solution)/shard_map/ppermute | solution.py:33
  62.2 16.4 %collective-permute-start.13 = (f32[16,4,1,128]{3,0,2,1:T(8,128)S(1)}, f32[16,4,1,128]{3,0,2,1:T(8,128)S(1)}, u32[]{:S(2)}, u32[]{:S(2)}) collective-permute-start(f32[16,4,1,128]{3,0,2,1:T(8,128)S(1)} %get-tuple-element.117), channel_id=1, source_target_pairs={{0,8},{8,16},{16,24},{24,32},{32,40},{40,48},{48,56},{56,64},{64,7... | collective-permute-start | bytes 98312 | tf_op jit(solution)/shard_map/ppermute | solution.py:33
  79.4 15.5 %collective-permute-start.17 = (f32[16,4,1,128]{3,0,2,1:T(8,128)S(1)}, f32[16,4,1,128]{3,0,2,1:T(8,128)S(1)}, u32[]{:S(2)}, u32[]{:S(2)}) collective-permute-start(f32[16,4,1,128]{3,0,2,1:T(8,128)S(1)} %get-tuple-element.113), channel_id=1, source_target_pairs={{0,8},{8,16},{16,24},{24,32},{32,40},{40,48},{48,56},{56,64},{64,7... | collective-permute-start | bytes 98312 | tf_op jit(solution)/shard_map/ppermute | solution.py:33
  97.5 235.9 %all-gather.13.cloned.1.call-start = ((), (), s32[]{:S(2)}) async-start(), calls=%async_computation.1 | async-start | bytes 5283840 | tf_op jit(solution)/shard_map/all_gather | solution.py:93
  192.9 13.7 %collective-permute-start.21 = (f32[16,4,1,128]{3,0,2,1:T(8,128)S(1)}, f32[16,4,1,128]{3,0,2,1:T(8,128)S(1)}, u32[]{:S(2)}, u32[]{:S(2)}) collective-permute-start(f32[16,4,1,128]{3,0,2,1:T(8,128)S(1)} %get-tuple-element.109), channel_id=1, source_target_pairs={{0,8},{8,16},{16,24},{24,32},{32,40},{40,48},{48,56},{56,64},{64,7... | collective-permute-start | bytes 98312 | tf_op jit(solution)/shard_map/ppermute | solution.py:33
  194.7 11.9 %collective-permute-start.22 = (f32[16,4,1,128]{3,0,2,1:T(8,128)S(1)}, f32[16,4,1,128]{3,0,2,1:T(8,128)S(1)}, u32[]{:S(2)}, u32[]{:S(2)}) collective-permute-start(f32[16,4,1,128]{3,0,2,1:T(8,128)S(1)} %get-tuple-element.110), channel_id=1, source_target_pairs={{8,0},{16,8},{24,16},{32,24},{40,32},{48,40},{56,48},{64,56},{72,6... | collective-permute-start | bytes 98312 | tf_op jit(solution)/shard_map/ppermute | solution.py:33
  207.4 15.5 %collective-permute-start.25 = (f32[16,4,1,128]{3,0,2,1:T(8,128)S(1)}, f32[16,4,1,128]{3,0,2,1:T(8,128)S(1)}, u32[]{:S(2)}, u32[]{:S(2)}) collective-permute-start(f32[16,4,1,128]{3,0,2,1:T(8,128)S(1)} %get-tuple-element.105), channel_id=1, source_target_pairs={{0,8},{8,16},{16,24},{24,32},{32,40},{40,48},{48,56},{56,64},{64,7... | collective-permute-start | bytes 98312 | tf_op jit(solution)/shard_map/ppermute | solution.py:33
  223.7 15.5 %collective-permute-start.29 = (f32[16,4,1,128]{3,0,2,1:T(8,128)S(1)}, f32[16,4,1,128]{3,0,2,1:T(8,128)S(1)}, u32[]{:S(2)}, u32[]{:S(2)}) collective-permute-start(f32[16,4,1,128]{3,0,2,1:T(8,128)S(1)} %get-tuple-element.101), channel_id=1, source_target_pairs={{0,8},{8,16},{16,24},{24,32},{32,40},{40,48},{48,56},{56,64},{64,7... | collective-permute-start | bytes 98312 | tf_op jit(solution)/shard_map/ppermute | solution.py:33
  240.0 15.5 %collective-permute-start.33 = (f32[16,4,1,128]{3,0,2,1:T(8,128)S(1)}, f32[16,4,1,128]{3,0,2,1:T(8,128)S(1)}, u32[]{:S(2)}, u32[]{:S(2)}) collective-permute-start(f32[16,4,1,128]{3,0,2,1:T(8,128)S(1)} %get-tuple-element.97), channel_id=1, source_target_pairs={{0,8},{8,16},{16,24},{24,32},{32,40},{40,48},{48,56},{56,64},{64,7... | collective-permute-start | bytes 98312 | tf_op jit(solution)/shard_map/ppermute | solution.py:33
  258.1 235.1 %all-gather.15.cloned.1.call-start = ((), (), s32[]{:S(2)}) async-start(), calls=%async_computation.2 | async-start | bytes 5283840 | tf_op jit(solution)/shard_map/all_gather | solution.py:93
  352.7 13.7 %collective-permute-start.37 = (f32[16,4,1,128]{3,0,2,1:T(8,128)S(1)}, f32[16,4,1,128]{3,0,2,1:T(8,128)S(1)}, u32[]{:S(2)}, u32[]{:S(2)}) collective-permute-start(f32[16,4,1,128]{3,0,2,1:T(8,128)S(1)} %get-tuple-element.93), channel_id=1, source_target_pairs={{0,8},{8,16},{16,24},{24,32},{32,40},{40,48},{48,56},{56,64},{64,7... | collective-permute-start | bytes 98312 | tf_op jit(solution)/shard_map/ppermute | solution.py:33
  354.5 11.9 %collective-permute-start.38 = (f32[16,4,1,128]{3,0,2,1:T(8,128)S(1)}, f32[16,4,1,128]{3,0,2,1:T(8,128)S(1)}, u32[]{:S(2)}, u32[]{:S(2)}) collective-permute-start(f32[16,4,1,128]{3,0,2,1:T(8,128)S(1)} %get-tuple-element.94), channel_id=1, source_target_pairs={{8,0},{16,8},{24,16},{32,24},{40,32},{48,40},{56,48},{64,56},{72,6... | collective-permute-start | bytes 98312 | tf_op jit(solution)/shard_map/ppermute | solution.py:33
  367.2 15.5 %collective-permute-start.41 = (f32[16,4,1,128]{3,0,2,1:T(8,128)S(1)}, f32[16,4,1,128]{3,0,2,1:T(8,128)S(1)}, u32[]{:S(2)}, u32[]{:S(2)}) collective-permute-start(f32[16,4,1,128]{3,0,2,1:T(8,128)S(1)} %get-tuple-element.89), channel_id=1, source_target_pairs={{0,8},{8,16},{16,24},{24,32},{32,40},{40,48},{48,56},{56,64},{64,7... | collective-permute-start | bytes 98312 | tf_op jit(solution)/shard_map/ppermute | solution.py:33
  371.5 11.2 %collective-permute-start.42 = (f32[16,4,1,128]{3,0,2,1:T(8,128)S(1)}, f32[16,4,1,128]{3,0,2,1:T(8,128)S(1)}, u32[]{:S(2)}, u32[]{:S(2)}) collective-permute-start(f32[16,4,1,128]{3,0,2,1:T(8,128)S(1)} %get-tuple-element.90), channel_id=1, source_target_pairs={{8,0},{16,8},{24,16},{32,24},{40,32},{48,40},{56,48},{64,56},{72,6... | collective-permute-start | bytes 98312 | tf_op jit(solution)/shard_map/ppermute | solution.py:33
  383.5 15.5 %collective-permute-start.45 = (f32[16,4,1,128]{3,0,2,1:T(8,128)S(1)}, f32[16,4,1,128]{3,0,2,1:T(8,128)S(1)}, u32[]{:S(2)}, u32[]{:S(2)}) collective-permute-start(f32[16,4,1,128]{3,0,2,1:T(8,128)S(1)} %get-tuple-element.85), channel_id=1, source_target_pairs={{0,8},{8,16},{16,24},{24,32},{32,40},{40,48},{48,56},{56,64},{64,7... | collective-permute-start | bytes 98312 | tf_op jit(solution)/shard_map/ppermute | solution.py:33
  399.8 15.5 %collective-permute-start.49 = (f32[16,4,1,128]{3,0,2,1:T(8,128)S(1)}, f32[16,4,1,128]{3,0,2,1:T(8,128)S(1)}, u32[]{:S(2)}, u32[]{:S(2)}) collective-permute-start(f32[16,4,1,128]{3,0,2,1:T(8,128)S(1)} %get-tuple-element.81), channel_id=1, source_target_pairs={{0,8},{8,16},{16,24},{24,32},{32,40},{40,48},{48,56},{56,64},{64,7... | collective-permute-start | bytes 98312 | tf_op jit(solution)/shard_map/ppermute | solution.py:33
  417.9 235.1 %all-gather.17.cloned.1.call-start = ((), (), s32[]{:S(2)}) async-start(), calls=%async_computation.3 | async-start | bytes 5283840 | tf_op jit(solution)/shard_map/all_gather | solution.py:93
  512.5 13.7 %collective-permute-start.53 = (f32[16,4,1,128]{3,0,2,1:T(8,128)S(1)}, f32[16,4,1,128]{3,0,2,1:T(8,128)S(1)}, u32[]{:S(2)}, u32[]{:S(2)}) collective-permute-start(f32[16,4,1,128]{3,0,2,1:T(8,128)S(1)} %get-tuple-element.77), channel_id=1, source_target_pairs={{0,8},{8,16},{16,24},{24,32},{32,40},{40,48},{48,56},{56,64},{64,7... | collective-permute-start | bytes 98312 | tf_op jit(solution)/shard_map/ppermute | solution.py:33
  514.3 11.9 %collective-permute-start.54 = (f32[16,4,1,128]{3,0,2,1:T(8,128)S(1)}, f32[16,4,1,128]{3,0,2,1:T(8,128)S(1)}, u32[]{:S(2)}, u32[]{:S(2)}) collective-permute-start(f32[16,4,1,128]{3,0,2,1:T(8,128)S(1)} %get-tuple-element.78), channel_id=1, source_target_pairs={{8,0},{16,8},{24,16},{32,24},{40,32},{48,40},{56,48},{64,56},{72,6... | collective-permute-start | bytes 98312 | tf_op jit(solution)/shard_map/ppermute | solution.py:33
  527.0 15.5 %collective-permute-start.57 = (f32[16,4,1,128]{3,0,2,1:T(8,128)S(1)}, f32[16,4,1,128]{3,0,2,1:T(8,128)S(1)}, u32[]{:S(2)}, u32[]{:S(2)}) collective-permute-start(f32[16,4,1,128]{3,0,2,1:T(8,128)S(1)} %get-tuple-element.73), channel_id=1, source_target_pairs={{0,8},{8,16},{16,24},{24,32},{32,40},{40,48},{48,56},{56,64},{64,7... | collective-permute-start | bytes 98312 | tf_op jit(solution)/shard_map/ppermute | solution.py:33
  543.3 15.5 %collective-permute-start.61 = (f32[16,4,1,128]{3,0,2,1:T(8,128)S(1)}, f32[16,4,1,128]{3,0,2,1:T(8,128)S(1)}, u32[]{:S(2)}, u32[]{:S(2)}) collective-permute-start(f32[16,4,1,128]{3,0,2,1:T(8,128)S(1)} %get-tuple-element.69), channel_id=1, source_target_pairs={{0,8},{8,16},{16,24},{24,32},{32,40},{40,48},{48,56},{56,64},{64,7... | collective-permute-start | bytes 98312 | tf_op jit(solution)/shard_map/ppermute | solution.py:33
  559.6 15.5 %collective-permute-start.65 = (f32[16,4,1,128]{3,0,2,1:T(8,128)S(1)}, f32[16,4,1,128]{3,0,2,1:T(8,128)S(1)}, u32[]{:S(2)}, u32[]{:S(2)}) collective-permute-start(f32[16,4,1,128]{3,0,2,1:T(8,128)S(1)} %get-tuple-element.65), channel_id=1, source_target_pairs={{0,8},{8,16},{16,24},{24,32},{32,40},{40,48},{48,56},{56,64},{64,7... | collective-permute-start | bytes 98312 | tf_op jit(solution)/shard_map/ppermute | solution.py:33
  577.7 235.5 %all-gather.19.cloned.1.call-start = ((), (), s32[]{:S(2)}) async-start(), calls=%async_computation.4 | async-start | bytes 5283840 | tf_op jit(solution)/shard_map/all_gather | solution.py:93
  672.6 13.7 %collective-permute-start.69 = (f32[16,4,1,128]{3,0,2,1:T(8,128)S(1)}, f32[16,4,1,128]{3,0,2,1:T(8,128)S(1)}, u32[]{:S(2)}, u32[]{:S(2)}) collective-permute-start(f32[16,4,1,128]{3,0,2,1:T(8,128)S(1)} %get-tuple-element.61), channel_id=1, source_target_pairs={{0,8},{8,16},{16,24},{24,32},{32,40},{40,48},{48,56},{56,64},{64,7... | collective-permute-start | bytes 98312 | tf_op jit(solution)/shard_map/ppermute | solution.py:33
  674.4 11.9 %collective-permute-start.70 = (f32[16,4,1,128]{3,0,2,1:T(8,128)S(1)}, f32[16,4,1,128]{3,0,2,1:T(8,128)S(1)}, u32[]{:S(2)}, u32[]{:S(2)}) collective-permute-start(f32[16,4,1,128]{3,0,2,1:T(8,128)S(1)} %get-tuple-element.62), channel_id=1, source_target_pairs={{8,0},{16,8},{24,16},{32,24},{40,32},{48,40},{56,48},{64,56},{72,6... | collective-permute-start | bytes 98312 | tf_op jit(solution)/shard_map/ppermute | solution.py:33
  687.2 15.5 %collective-permute-start.73 = (f32[16,4,1,128]{3,0,2,1:T(8,128)S(1)}, f32[16,4,1,128]{3,0,2,1:T(8,128)S(1)}, u32[]{:S(2)}, u32[]{:S(2)}) collective-permute-start(f32[16,4,1,128]{3,0,2,1:T(8,128)S(1)} %get-tuple-element.57), channel_id=1, source_target_pairs={{0,8},{8,16},{16,24},{24,32},{32,40},{40,48},{48,56},{56,64},{64,7... | collective-permute-start | bytes 98312 | tf_op jit(solution)/shard_map/ppermute | solution.py:33
  691.5 11.2 %collective-permute-start.74 = (f32[16,4,1,128]{3,0,2,1:T(8,128)S(1)}, f32[16,4,1,128]{3,0,2,1:T(8,128)S(1)}, u32[]{:S(2)}, u32[]{:S(2)}) collective-permute-start(f32[16,4,1,128]{3,0,2,1:T(8,128)S(1)} %get-tuple-element.58), channel_id=1, source_target_pairs={{8,0},{16,8},{24,16},{32,24},{40,32},{48,40},{56,48},{64,56},{72,6... | collective-permute-start | bytes 98312 | tf_op jit(solution)/shard_map/ppermute | solution.py:33
  703.5 15.5 %collective-permute-start.77 = (f32[16,4,1,128]{3,0,2,1:T(8,128)S(1)}, f32[16,4,1,128]{3,0,2,1:T(8,128)S(1)}, u32[]{:S(2)}, u32[]{:S(2)}) collective-permute-start(f32[16,4,1,128]{3,0,2,1:T(8,128)S(1)} %get-tuple-element.53), channel_id=1, source_target_pairs={{0,8},{8,16},{16,24},{24,32},{32,40},{40,48},{48,56},{56,64},{64,7... | collective-permute-start | bytes 98312 | tf_op jit(solution)/shard_map/ppermute | solution.py:33
  719.8 15.5 %collective-permute-start.81 = (f32[16,4,1,128]{3,0,2,1:T(8,128)S(1)}, f32[16,4,1,128]{3,0,2,1:T(8,128)S(1)}, u32[]{:S(2)}, u32[]{:S(2)}) collective-permute-start(f32[16,4,1,128]{3,0,2,1:T(8,128)S(1)} %get-tuple-element.49), channel_id=1, source_target_pairs={{0,8},{8,16},{16,24},{24,32},{32,40},{40,48},{48,56},{56,64},{64,7... | collective-permute-start | bytes 98312 | tf_op jit(solution)/shard_map/ppermute | solution.py:33
  (83 other events, 670.1 us)
Sparse Core Ops, SparseCore 0:
  97.6 75.9 all-gather.10
  258.2 75.1 all-gather.12
  418.0 75.1 all-gather.14
  577.8 75.1 all-gather.16
  738.0 75.1 all-gather.18
